TPU v7x, 256 devices: a whole 4x4x8 slice. The times are simulated.
256 devices in a mesh: gx: 4 (over y), gy: 16 (over z, x_lo), ma: 4 (over x_hi, core).
Axes of the slice: x: 4 (x_hi: 2, x_lo: 2; x = x_hi * 2 + x_lo), y: 4, z: 8, core: 2. Of those that a mesh axis runs over, the one named last changes fastest.
Arguments:
- control: float32 [33, 256, 2048], P(None, 'gx', 'gy'), may hold values from -6 to 6
- perturb: bfloat16 [16, 33, 256, 2048], P('ma', None, 'gx', 'gy'), may hold values from -6 to 6
- weights: float32 [16, 256, 2048], P('ma', 'gx', 'gy'), may hold values from -6 to 6
- kappa: float32 [4, 256, 2048], P(None, 'gx', 'gy'), may hold values from 0.2 to 0.49
- wet_levels: int32 [256, 2048], P('gx', 'gy'), may hold values from 0 to 31
- obs_index: int32 [131072], P(('gx', 'gy')), may hold values from 0 to 270335, as said below
- obs_count: int32 [64], P(('gx', 'gy')), may hold values from 1024 to 2048, as said below
- innov: float32 [131072], P(('gx', 'gy')), may hold values from -6 to 6
- obs_weight: float32 [131072], P(('gx', 'gy')), may hold values from 0.25 to 4
Outputs:
- grad_control: float32 [33, 256, 2048], P(None, 'gx', 'gy')
- grad_weights: float32 [16, 256, 2048], P('ma', 'gx', 'gy')
Inputs may be any that keep to these rules, and one draw needn't show every extreme that they name: `obs_index`: index p * 64 * 128 + i * 128 + j of a cell of plane p, local longitude i and local latitude j within the observation's tile; several slots may name the same cell. `obs_count`: the live slots of a tile are its first ones. Column (i, j) is wet at level l when l < wet_levels[i, j].
All inputs are finite; a program needn't handle non-finite values.
Results may differ from a plain program's by a relative error of at most 0.0003.
Values sent between devices are 32-bit elements; how exact they have to be, the bound alone decides.
A program may use at most 64 MiB of HBM per device.

v0:
```python
import math

import jax
import jax.numpy as jnp
from jax import lax
from jax.sharding import PartitionSpec as P

NSTEP = 10
LSTEP = 4


def passed_along(value, axis, steps):
    count = lax.axis_size(axis)
    pairs = [(source, (source + steps) % count) for source in range(count)]
    return lax.ppermute(value, axis, pairs)


def shifted(value, axis, steps):
    count = lax.axis_size(axis)
    initial, last = (max(0, -steps), min(count, count - steps))
    return lax.ppermute(value, axis, [(source, source + steps) for source in range(initial, last)])


def neighbours(field):
    rows = field.shape[1]
    columns = field.shape[2]
    east_edge = passed_along(field[:, :1, :], "gx", -1)
    west_edge = passed_along(field[:, rows - 1 :, :], "gx", 1)
    north_edge = shifted(field[:, :, :1], "gy", -1)
    south_edge = shifted(field[:, :, columns - 1 :], "gy", 1)
    row_iota = lax.broadcasted_iota(jnp.int32, field.shape, 1)
    column_iota = lax.broadcasted_iota(jnp.int32, field.shape, 2)
    east = jnp.where(row_iota == rows - 1, east_edge, jnp.roll(field, -1, axis=1))
    west = jnp.where(row_iota == 0, west_edge, jnp.roll(field, 1, axis=1))
    north = jnp.where(column_iota == columns - 1, north_edge, jnp.roll(field, -1, axis=2))
    south = jnp.where(column_iota == 0, south_edge, jnp.roll(field, 1, axis=2))
    return (east, west, north, south)


def local_step(field, faces):
    east_face, west_face, north_face, south_face = faces
    east, west, north, south = neighbours(field)
    change_x = east_face * (east - field) - west_face * (field - west)
    change_y = north_face * (north - field) - south_face * (field - south)
    return field + change_x + change_y


def diffuse(field, faces, count):
    return lax.fori_loop(0, count, lambda index, current: local_step(current, faces), field)


def on_device(
    control, perturb, weights, kappa, wet_levels, obs_index, obs_count, innov, obs_weight
):
    planes, cells_x, cells_y = control.shape
    levels = (planes - 1) // 2
    level_iota = lax.broadcasted_iota(jnp.int32, (levels, 1, 1), 0)
    wet_mask = (level_iota < wet_levels[None]).astype(jnp.float32)
    surface = wet_mask[0:1]
    coef = jnp.concatenate(
        [kappa[0:1] * wet_mask, kappa[1:2] * wet_mask, kappa[2:3] * surface, kappa[3:4] * surface],
        axis=0,
    )
    coef_east, coef_west, coef_north, coef_south = neighbours(coef)
    all_faces = (coef * coef_east, coef_west * coef, coef * coef_north, coef_south * coef)
    static_faces = tuple((face[:planes] for face in all_faces))
    local_faces = tuple((face[planes:] for face in all_faces))
    member_scale = 1.0 / math.sqrt(perturb.shape[0] * lax.axis_size("ma"))
    plane_cells = cells_x * cells_y
    static = diffuse(control, static_faces, NSTEP)
    static_seen = static.reshape(-1)[obs_index]
    local = diffuse(weights, local_faces, LSTEP)
    partial_sum = member_scale * jnp.sum(perturb.astype(jnp.float32) * local[:, None], axis=0)
    summed = lax.psum(partial_sum, "ma")
    ensemble_seen = summed.reshape(-1)[obs_index]
    observed = static_seen + ensemble_seen
    live_obs = lax.broadcasted_iota(jnp.int32, obs_index.shape, 0) < obs_count[0]
    misfit = obs_weight * (observed - innov)
    resid = jnp.where(live_obs, misfit, jnp.zeros_like(misfit))
    adjoint = jnp.zeros((planes * plane_cells,), jnp.float32).at[obs_index].add(resid)
    adjoint = adjoint.reshape(planes, cells_x, cells_y)
    grad_control = control + diffuse(adjoint, static_faces, NSTEP)
    project = member_scale * jnp.sum(perturb.astype(jnp.float32) * adjoint[None], axis=1)
    grad_weights = weights + diffuse(project, local_faces, LSTEP)
    return (grad_control, grad_weights)


def solution(mesh):
    placed = (
        P(None, "gx", "gy"),
        P("ma", None, "gx", "gy"),
        P("ma", "gx", "gy"),
        P(None, "gx", "gy"),
        P("gx", "gy"),
        P(("gx", "gy")),
        P(("gx", "gy")),
        P(("gx", "gy")),
        P(("gx", "gy")),
    )
    return jax.shard_map(
        on_device,
        mesh=mesh,
        in_specs=placed,
        out_specs=(P(None, "gx", "gy"), P("ma", "gx", "gy")),
        check_vma=False,
    )
```

profile of v0, /device:TPU:126, one launch (start us, length us, event | category | flops | bytes accessed | tf_op | source)
XLA Modules:
  0.0 851.5 jit_solution(10855238930807510192)
XLA Ops:
  48.4 92.3 %while.41 = (s32[]{:T(128)}, f32[4,64,128]{1,0,2:T(4,128)S(1)}, f32[1,64,128]{1,2,0:T(8,128)S(1)}, f32[1,64,128]{1,2,0:T(8,128)}, f32[1,64,128]{1,2,0:T(8,128)}, /*index=5*/f32[1,64,128]{1,2,0:T(8,128)S(1)}, s32[]{:T(128)}) while((s32[]{:T(128)}, f32[4,64,128]{1,0,2:T(4,128)S(1)}, f32[1,64,128]{1,2,0:T(8,128)S(1)}, f32[1,64,128]{1,2,0:T(8,128)}, ...), condition=%wide.region_3.4_spmd, body=%wide.region_2.3_spmd.sunk | while | flops 655746 | bytes 2014189 | solution.py:49
  50.3 6.0 collective-permute-start.4
  73.4 6.0 collective-permute-start.4
  96.5 6.0 collective-permute-start.4
  119.6 6.0 collective-permute-start.4
  144.2 265.4 %while.40 = (s32[]{:T(128)}, f32[33,64,128]{2,0,1:T(8,128)S(1)}, f32[33,64,128]{2,0,1:T(8,128)}, f32[33,64,128]{2,0,1:T(8,128)}, f32[33,64,128]{2,0,1:T(8,128)}, /*index=5*/f32[33,64,128]{2,0,1:T(8,128)S(1)}, s32[]{:T(128)}) while((s32[]{:T(128)}, f32[33,64,128]{2,0,1:T(8,128)S(1)}, f32[33,64,128]{2,0,1:T(8,128)}, f32[33,64,128]{2,0,1:T(8,128)}, ...), condition=%wide.region_1.2_spmd, body=%wide.region_0.1_spmd.sunk | while | flops 5407106 | bytes 21948908 | solution.py:49
  152.3 6.0 collective-permute-start
  178.9 6.0 collective-permute-start
  205.5 6.0 collective-permute-start
  232.0 6.0 collective-permute-start
  258.5 6.0 collective-permute-start
  285.0 6.0 collective-permute-start
  311.6 6.0 collective-permute-start
  338.1 6.0 collective-permute-start
  364.6 6.0 collective-permute-start
  391.2 6.0 collective-permute-start
  410.8 26.3 %gather_fusion = f32[2048]{0:T(1024)S(1)} fusion(f32[270336]{0:T(1024)} %bitcast.95, s32[2048]{0:T(1024)S(1)} %copy-done.7), kind=kCustom, calls=%fused_computation | custom fusion | bytes 24576 | tf_op jit(solution)/shard_map/gather | solution.py:71
  437.1 24.5 %gather_fusion.1 = f32[2048]{0:T(1024)S(1)} fusion(f32[270336]{0:T(1024)} %all-reduce.2.cloned.1.call-done, s32[2048]{0:T(1024)S(1)} %copy-done.7), kind=kCustom, calls=%fused_computation.1 | custom fusion | bytes 24576 | tf_op jit(solution)/shard_map/gather | solution.py:75
  461.7 11.9 %scatter_custom_fusion = f32[270336]{0:T(1024)S(1)} fusion(s32[2048]{0:T(1024)} %get-tuple-element.317, f32[2048]{0:T(1024)S(1)} %multiply_select_fusion, f32[]{:T(128)} %constant.23.clone.1), kind=kCustom, calls=%fused_computation.98 | custom fusion | flops 2048 | bytes 1081856 | tf_op jit(solution)/shard_map/scatter-add | solution.py:80
  478.7 96.6 %while.43 = (s32[]{:T(128)}, f32[4,64,128]{1,0,2:T(4,128)S(1)}, f32[1,64,128]{1,2,0:T(8,128)S(1)}, f32[1,64,128]{1,2,0:T(8,128)}, f32[1,64,128]{1,2,0:T(8,128)}, /*index=5*/f32[1,64,128]{1,2,0:T(8,128)S(1)}, s32[]{:T(128)}) while((s32[]{:T(128)}, f32[4,64,128]{1,0,2:T(4,128)S(1)}, f32[1,64,128]{1,2,0:T(8,128)S(1)}, ...), condition=%wide.region_11.12_spmd, body=%wide.region_10.11_spmd.sunk | while | flops 655746 | bytes 2014189 | solution.py:49
  480.6 6.0 collective-permute-start.12
  505.9 6.0 collective-permute-start.12
  530.7 6.0 collective-permute-start.12
  554.2 6.0 collective-permute-start.12
  577.0 265.2 %while.42 = (s32[]{:T(128)}, f32[33,64,128]{2,0,1:T(8,128)S(1)}, f32[33,64,128]{2,0,1:T(8,128)}, f32[33,64,128]{2,0,1:T(8,128)}, f32[33,64,128]{2,0,1:T(8,128)}, /*index=5*/f32[33,64,128]{2,0,1:T(8,128)S(1)}, s32[]{:T(128)}) while((s32[]{:T(128)}, f32[33,64,128]{2,0,1:T(8,128)S(1)}, f32[33,64,128]{2,0,1:T(8,128)}, f32[33,64,128]{2,0,1:T(8,128)}, ...), condition=%wide.region_8.9_spmd, body=%wide.region_7.8_spmd.sunk | while | flops 5407106 | bytes 21948908 | solution.py:49
  585.0 6.0 collective-permute-start.8
  611.6 6.0 collective-permute-start.8
  638.1 6.0 collective-permute-start.8
  664.6 6.0 collective-permute-start.8
  691.1 6.0 collective-permute-start.8
  717.7 6.0 collective-permute-start.8
  744.2 6.0 collective-permute-start.8
  (602 shorter events, 621.2 us)
Async XLA Ops:
  7.2 430.0 %all-reduce.2.cloned.1.call-start = ((), (), s32[]{:S(2)}) async-start(), calls=%async_computation | async-start | bytes 2162688 | tf_op jit(solution)/shard_map/psum | solution.py:74
  10.6 30.6 %collective-permute-start.17 = (f32[34,1,128]{2,0,1:T(8,128)}, f32[34,1,128]{2,0,1:T(8,128)}, u32[]{:S(2)}, u32[]{:S(2)}) collective-permute-start(f32[34,1,128]{2,0,1:T(8,128)} %get-tuple-element.300), channel_id=1, source_target_pairs={{0,64},{64,128},{128,192},{192,0},{1,65},{65,129},{129,193},{193,1... | collective-permute-start | bytes 52232 | tf_op jit(solution)/shard_map/ppermute | solution.py:15
  10.8 24.0 %collective-permute-start.16 = (f32[34,1,128]{2,0,1:T(8,128)S(1)}, f32[34,1,128]{2,0,1:T(8,128)S(1)}, u32[]{:S(2)}, u32[]{:S(2)}) collective-permute-start(f32[34,1,128]{2,0,1:T(8,128)S(1)} %get-tuple-element.301), channel_id=1, source_target_pairs={{0,192},{64,0},{128,64},{192,128},{1,193},{65,1},{129,65},{193,129... | collective-permute-start | bytes 52232 | tf_op jit(solution)/shard_map/ppermute | solution.py:15
  144.2 21.1 %collective-permute-start.3 = (f32[33,1,128]{2,0,1:T(8,128)S(1)}, f32[33,1,128]{2,0,1:T(8,128)S(1)}, u32[]{:S(2)}, u32[]{:S(2)}) collective-permute-start(f32[33,1,128]{2,0,1:T(8,128)S(1)} %get-tuple-element.496), channel_id=1, source_target_pairs={{0,192},{64,0},{128,64},{192,128},{1,193},{65,1},{129,65},{193,129... | collective-permute-start | bytes 50696 | tf_op jit(solution)/shard_map/while/body/eval_jaxpr/ppermute | solution.py:15
  144.3 21.1 %collective-permute-start.2 = (f32[33,1,128]{2,0,1:T(8,128)S(1)}, f32[33,1,128]{2,0,1:T(8,128)S(1)}, u32[]{:S(2)}, u32[]{:S(2)}) collective-permute-start(f32[33,1,128]{2,0,1:T(8,128)S(1)} %get-tuple-element.499), channel_id=1, source_target_pairs={{0,64},{64,128},{128,192},{192,0},{1,65},{65,129},{129,193},{193,1... | collective-permute-start | bytes 50696 | tf_op jit(solution)/shard_map/while/body/eval_jaxpr/ppermute | solution.py:15
  170.8 21.2 %collective-permute-start.3 = (f32[33,1,128]{2,0,1:T(8,128)S(1)}, f32[33,1,128]{2,0,1:T(8,128)S(1)}, u32[]{:S(2)}, u32[]{:S(2)}) collective-permute-start(f32[33,1,128]{2,0,1:T(8,128)S(1)} %get-tuple-element.496), channel_id=1, source_target_pairs={{0,192},{64,0},{128,64},{192,128},{1,193},{65,1},{129,65},{193,129... | collective-permute-start | bytes 50696 | tf_op jit(solution)/shard_map/while/body/eval_jaxpr/ppermute | solution.py:15
  170.9 21.1 %collective-permute-start.2 = (f32[33,1,128]{2,0,1:T(8,128)S(1)}, f32[33,1,128]{2,0,1:T(8,128)S(1)}, u32[]{:S(2)}, u32[]{:S(2)}) collective-permute-start(f32[33,1,128]{2,0,1:T(8,128)S(1)} %get-tuple-element.499), channel_id=1, source_target_pairs={{0,64},{64,128},{128,192},{192,0},{1,65},{65,129},{129,193},{193,1... | collective-permute-start | bytes 50696 | tf_op jit(solution)/shard_map/while/body/eval_jaxpr/ppermute | solution.py:15
  197.4 21.1 %collective-permute-start.3 = (f32[33,1,128]{2,0,1:T(8,128)S(1)}, f32[33,1,128]{2,0,1:T(8,128)S(1)}, u32[]{:S(2)}, u32[]{:S(2)}) collective-permute-start(f32[33,1,128]{2,0,1:T(8,128)S(1)} %get-tuple-element.496), channel_id=1, source_target_pairs={{0,192},{64,0},{128,64},{192,128},{1,193},{65,1},{129,65},{193,129... | collective-permute-start | bytes 50696 | tf_op jit(solution)/shard_map/while/body/eval_jaxpr/ppermute | solution.py:15
  197.5 21.0 %collective-permute-start.2 = (f32[33,1,128]{2,0,1:T(8,128)S(1)}, f32[33,1,128]{2,0,1:T(8,128)S(1)}, u32[]{:S(2)}, u32[]{:S(2)}) collective-permute-start(f32[33,1,128]{2,0,1:T(8,128)S(1)} %get-tuple-element.499), channel_id=1, source_target_pairs={{0,64},{64,128},{128,192},{192,0},{1,65},{65,129},{129,193},{193,1... | collective-permute-start | bytes 50696 | tf_op jit(solution)/shard_map/while/body/eval_jaxpr/ppermute | solution.py:15
  223.9 21.1 %collective-permute-start.3 = (f32[33,1,128]{2,0,1:T(8,128)S(1)}, f32[33,1,128]{2,0,1:T(8,128)S(1)}, u32[]{:S(2)}, u32[]{:S(2)}) collective-permute-start(f32[33,1,128]{2,0,1:T(8,128)S(1)} %get-tuple-element.496), channel_id=1, source_target_pairs={{0,192},{64,0},{128,64},{192,128},{1,193},{65,1},{129,65},{193,129... | collective-permute-start | bytes 50696 | tf_op jit(solution)/shard_map/while/body/eval_jaxpr/ppermute | solution.py:15
  250.4 21.1 %collective-permute-start.3 = (f32[33,1,128]{2,0,1:T(8,128)S(1)}, f32[33,1,128]{2,0,1:T(8,128)S(1)}, u32[]{:S(2)}, u32[]{:S(2)}) collective-permute-start(f32[33,1,128]{2,0,1:T(8,128)S(1)} %get-tuple-element.496), channel_id=1, source_target_pairs={{0,192},{64,0},{128,64},{192,128},{1,193},{65,1},{129,65},{193,129... | collective-permute-start | bytes 50696 | tf_op jit(solution)/shard_map/while/body/eval_jaxpr/ppermute | solution.py:15
  250.5 21.0 %collective-permute-start.2 = (f32[33,1,128]{2,0,1:T(8,128)S(1)}, f32[33,1,128]{2,0,1:T(8,128)S(1)}, u32[]{:S(2)}, u32[]{:S(2)}) collective-permute-start(f32[33,1,128]{2,0,1:T(8,128)S(1)} %get-tuple-element.499), channel_id=1, source_target_pairs={{0,64},{64,128},{128,192},{192,0},{1,65},{65,129},{129,193},{193,1... | collective-permute-start | bytes 50696 | tf_op jit(solution)/shard_map/while/body/eval_jaxpr/ppermute | solution.py:15
  277.0 21.1 %collective-permute-start.3 = (f32[33,1,128]{2,0,1:T(8,128)S(1)}, f32[33,1,128]{2,0,1:T(8,128)S(1)}, u32[]{:S(2)}, u32[]{:S(2)}) collective-permute-start(f32[33,1,128]{2,0,1:T(8,128)S(1)} %get-tuple-element.496), channel_id=1, source_target_pairs={{0,192},{64,0},{128,64},{192,128},{1,193},{65,1},{129,65},{193,129... | collective-permute-start | bytes 50696 | tf_op jit(solution)/shard_map/while/body/eval_jaxpr/ppermute | solution.py:15
  277.1 21.0 %collective-permute-start.2 = (f32[33,1,128]{2,0,1:T(8,128)S(1)}, f32[33,1,128]{2,0,1:T(8,128)S(1)}, u32[]{:S(2)}, u32[]{:S(2)}) collective-permute-start(f32[33,1,128]{2,0,1:T(8,128)S(1)} %get-tuple-element.499), channel_id=1, source_target_pairs={{0,64},{64,128},{128,192},{192,0},{1,65},{65,129},{129,193},{193,1... | collective-permute-start | bytes 50696 | tf_op jit(solution)/shard_map/while/body/eval_jaxpr/ppermute | solution.py:15
  303.5 21.1 %collective-permute-start.3 = (f32[33,1,128]{2,0,1:T(8,128)S(1)}, f32[33,1,128]{2,0,1:T(8,128)S(1)}, u32[]{:S(2)}, u32[]{:S(2)}) collective-permute-start(f32[33,1,128]{2,0,1:T(8,128)S(1)} %get-tuple-element.496), channel_id=1, source_target_pairs={{0,192},{64,0},{128,64},{192,128},{1,193},{65,1},{129,65},{193,129... | collective-permute-start | bytes 50696 | tf_op jit(solution)/shard_map/while/body/eval_jaxpr/ppermute | solution.py:15
  303.6 21.0 %collective-permute-start.2 = (f32[33,1,128]{2,0,1:T(8,128)S(1)}, f32[33,1,128]{2,0,1:T(8,128)S(1)}, u32[]{:S(2)}, u32[]{:S(2)}) collective-permute-start(f32[33,1,128]{2,0,1:T(8,128)S(1)} %get-tuple-element.499), channel_id=1, source_target_pairs={{0,64},{64,128},{128,192},{192,0},{1,65},{65,129},{129,193},{193,1... | collective-permute-start | bytes 50696 | tf_op jit(solution)/shard_map/while/body/eval_jaxpr/ppermute | solution.py:15
  330.0 21.1 %collective-permute-start.3 = (f32[33,1,128]{2,0,1:T(8,128)S(1)}, f32[33,1,128]{2,0,1:T(8,128)S(1)}, u32[]{:S(2)}, u32[]{:S(2)}) collective-permute-start(f32[33,1,128]{2,0,1:T(8,128)S(1)} %get-tuple-element.496), channel_id=1, source_target_pairs={{0,192},{64,0},{128,64},{192,128},{1,193},{65,1},{129,65},{193,129... | collective-permute-start | bytes 50696 | tf_op jit(solution)/shard_map/while/body/eval_jaxpr/ppermute | solution.py:15
  356.5 21.1 %collective-permute-start.3 = (f32[33,1,128]{2,0,1:T(8,128)S(1)}, f32[33,1,128]{2,0,1:T(8,128)S(1)}, u32[]{:S(2)}, u32[]{:S(2)}) collective-permute-start(f32[33,1,128]{2,0,1:T(8,128)S(1)} %get-tuple-element.496), channel_id=1, source_target_pairs={{0,192},{64,0},{128,64},{192,128},{1,193},{65,1},{129,65},{193,129... | collective-permute-start | bytes 50696 | tf_op jit(solution)/shard_map/while/body/eval_jaxpr/ppermute | solution.py:15
  383.1 21.1 %collective-permute-start.3 = (f32[33,1,128]{2,0,1:T(8,128)S(1)}, f32[33,1,128]{2,0,1:T(8,128)S(1)}, u32[]{:S(2)}, u32[]{:S(2)}) collective-permute-start(f32[33,1,128]{2,0,1:T(8,128)S(1)} %get-tuple-element.496), channel_id=1, source_target_pairs={{0,192},{64,0},{128,64},{192,128},{1,193},{65,1},{129,65},{193,129... | collective-permute-start | bytes 50696 | tf_op jit(solution)/shard_map/while/body/eval_jaxpr/ppermute | solution.py:15
  478.7 21.7 %collective-permute-start.13 = (f32[4,64,1]{1,0,2:T(4,128)S(1)}, f32[4,64,1]{1,0,2:T(4,128)S(1)}, u32[]{:S(2)}, u32[]{:S(2)}) collective-permute-start(f32[4,64,1]{1,0,2:T(4,128)S(1)} %get-tuple-element.554), channel_id=1, source_target_pairs={{4,0},{8,4},{12,8},{16,12},{20,16},{24,20},{28,24},{32,28},{36,32}... | collective-permute-start | bytes 3080 | tf_op jit(solution)/shard_map/while/body/eval_jaxpr/ppermute | solution.py:21
  504.0 21.3 %collective-permute-start.13 = (f32[4,64,1]{1,0,2:T(4,128)S(1)}, f32[4,64,1]{1,0,2:T(4,128)S(1)}, u32[]{:S(2)}, u32[]{:S(2)}) collective-permute-start(f32[4,64,1]{1,0,2:T(4,128)S(1)} %get-tuple-element.554), channel_id=1, source_target_pairs={{4,0},{8,4},{12,8},{16,12},{20,16},{24,20},{28,24},{32,28},{36,32}... | collective-permute-start | bytes 3080 | tf_op jit(solution)/shard_map/while/body/eval_jaxpr/ppermute | solution.py:21
  577.0 21.0 %collective-permute-start.11 = (f32[33,1,128]{2,0,1:T(8,128)S(1)}, f32[33,1,128]{2,0,1:T(8,128)S(1)}, u32[]{:S(2)}, u32[]{:S(2)}) collective-permute-start(f32[33,1,128]{2,0,1:T(8,128)S(1)} %get-tuple-element.532), channel_id=1, source_target_pairs={{0,192},{64,0},{128,64},{192,128},{1,193},{65,1},{129,65},{193,129... | collective-permute-start | bytes 50696 | tf_op jit(solution)/shard_map/while/body/eval_jaxpr/ppermute | solution.py:15
  577.0 21.0 %collective-permute-start.10 = (f32[33,1,128]{2,0,1:T(8,128)S(1)}, f32[33,1,128]{2,0,1:T(8,128)S(1)}, u32[]{:S(2)}, u32[]{:S(2)}) collective-permute-start(f32[33,1,128]{2,0,1:T(8,128)S(1)} %get-tuple-element.535), channel_id=1, source_target_pairs={{0,64},{64,128},{128,192},{192,0},{1,65},{65,129},{129,193},{193,1... | collective-permute-start | bytes 50696 | tf_op jit(solution)/shard_map/while/body/eval_jaxpr/ppermute | solution.py:15
  603.5 21.1 %collective-permute-start.11 = (f32[33,1,128]{2,0,1:T(8,128)S(1)}, f32[33,1,128]{2,0,1:T(8,128)S(1)}, u32[]{:S(2)}, u32[]{:S(2)}) collective-permute-start(f32[33,1,128]{2,0,1:T(8,128)S(1)} %get-tuple-element.532), channel_id=1, source_target_pairs={{0,192},{64,0},{128,64},{192,128},{1,193},{65,1},{129,65},{193,129... | collective-permute-start | bytes 50696 | tf_op jit(solution)/shard_map/while/body/eval_jaxpr/ppermute | solution.py:15
  630.0 21.1 %collective-permute-start.11 = (f32[33,1,128]{2,0,1:T(8,128)S(1)}, f32[33,1,128]{2,0,1:T(8,128)S(1)}, u32[]{:S(2)}, u32[]{:S(2)}) collective-permute-start(f32[33,1,128]{2,0,1:T(8,128)S(1)} %get-tuple-element.532), channel_id=1, source_target_pairs={{0,192},{64,0},{128,64},{192,128},{1,193},{65,1},{129,65},{193,129... | collective-permute-start | bytes 50696 | tf_op jit(solution)/shard_map/while/body/eval_jaxpr/ppermute | solution.py:15
  656.5 21.1 %collective-permute-start.11 = (f32[33,1,128]{2,0,1:T(8,128)S(1)}, f32[33,1,128]{2,0,1:T(8,128)S(1)}, u32[]{:S(2)}, u32[]{:S(2)}) collective-permute-start(f32[33,1,128]{2,0,1:T(8,128)S(1)} %get-tuple-element.532), channel_id=1, source_target_pairs={{0,192},{64,0},{128,64},{192,128},{1,193},{65,1},{129,65},{193,129... | collective-permute-start | bytes 50696 | tf_op jit(solution)/shard_map/while/body/eval_jaxpr/ppermute | solution.py:15
  683.1 21.1 %collective-permute-start.11 = (f32[33,1,128]{2,0,1:T(8,128)S(1)}, f32[33,1,128]{2,0,1:T(8,128)S(1)}, u32[]{:S(2)}, u32[]{:S(2)}) collective-permute-start(f32[33,1,128]{2,0,1:T(8,128)S(1)} %get-tuple-element.532), channel_id=1, source_target_pairs={{0,192},{64,0},{128,64},{192,128},{1,193},{65,1},{129,65},{193,129... | collective-permute-start | bytes 50696 | tf_op jit(solution)/shard_map/while/body/eval_jaxpr/ppermute | solution.py:15
  709.6 21.1 %collective-permute-start.11 = (f32[33,1,128]{2,0,1:T(8,128)S(1)}, f32[33,1,128]{2,0,1:T(8,128)S(1)}, u32[]{:S(2)}, u32[]{:S(2)}) collective-permute-start(f32[33,1,128]{2,0,1:T(8,128)S(1)} %get-tuple-element.532), channel_id=1, source_target_pairs={{0,192},{64,0},{128,64},{192,128},{1,193},{65,1},{129,65},{193,129... | collective-permute-start | bytes 50696 | tf_op jit(solution)/shard_map/while/body/eval_jaxpr/ppermute | solution.py:15
  736.1 21.1 %collective-permute-start.11 = (f32[33,1,128]{2,0,1:T(8,128)S(1)}, f32[33,1,128]{2,0,1:T(8,128)S(1)}, u32[]{:S(2)}, u32[]{:S(2)}) collective-permute-start(f32[33,1,128]{2,0,1:T(8,128)S(1)} %get-tuple-element.532), channel_id=1, source_target_pairs={{0,192},{64,0},{128,64},{192,128},{1,193},{65,1},{129,65},{193,129... | collective-permute-start | bytes 50696 | tf_op jit(solution)/shard_map/while/body/eval_jaxpr/ppermute | solution.py:15
  762.6 21.1 %collective-permute-start.11 = (f32[33,1,128]{2,0,1:T(8,128)S(1)}, f32[33,1,128]{2,0,1:T(8,128)S(1)}, u32[]{:S(2)}, u32[]{:S(2)}) collective-permute-start(f32[33,1,128]{2,0,1:T(8,128)S(1)} %get-tuple-element.532), channel_id=1, source_target_pairs={{0,192},{64,0},{128,64},{192,128},{1,193},{65,1},{129,65},{193,129... | collective-permute-start | bytes 50696 | tf_op jit(solution)/shard_map/while/body/eval_jaxpr/ppermute | solution.py:15
  789.2 21.1 %collective-permute-start.11 = (f32[33,1,128]{2,0,1:T(8,128)S(1)}, f32[33,1,128]{2,0,1:T(8,128)S(1)}, u32[]{:S(2)}, u32[]{:S(2)}) collective-permute-start(f32[33,1,128]{2,0,1:T(8,128)S(1)} %get-tuple-element.532), channel_id=1, source_target_pairs={{0,192},{64,0},{128,64},{192,128},{1,193},{65,1},{129,65},{193,129... | collective-permute-start | bytes 50696 | tf_op jit(solution)/shard_map/while/body/eval_jaxpr/ppermute | solution.py:15
  815.7 21.1 %collective-permute-start.11 = (f32[33,1,128]{2,0,1:T(8,128)S(1)}, f32[33,1,128]{2,0,1:T(8,128)S(1)}, u32[]{:S(2)}, u32[]{:S(2)}) collective-permute-start(f32[33,1,128]{2,0,1:T(8,128)S(1)} %get-tuple-element.532), channel_id=1, source_target_pairs={{0,192},{64,0},{128,64},{192,128},{1,193},{65,1},{129,65},{193,129... | collective-permute-start | bytes 50696 | tf_op jit(solution)/shard_map/while/body/eval_jaxpr/ppermute | solution.py:15
  (96 other events, 1383.5 us)
Sparse Core Ops, SparseCore 0:
  144.3 47.7 all-reduce.1
where the time goes:
time: 858 us; the launch traced here: 852 us
  starting transfers between devices  325 us (38%)
  local copies, waits for them, and re-layouts  316 us (37%)
  other arithmetic  177 us (21%)
  waiting for transfers between devices  16.9 us (2%)
  between operations  15 us (2%)
    ppermute x58, starting transfers between devices, shifted(): lax.ppermute(value, axis, [(source, source + steps) for source in range(i...  230 us
    add x28, other arithmetic, local_step(): return field + change_x + change_y  135 us
    ppermute x58, starting transfers between devices, passed_along(): return lax.ppermute(value, axis, pairs)  94.5 us
    slice x50, local copies, waits for them, and re-layouts, neighbours(): south_edge = shifted(field[:, :, columns - 1:], 'gy', 1)  50.6 us
    slice x29, local copies, waits for them, and re-layouts, neighbours(): south = jnp.where(column_iota == 0, south_edge, jnp.roll(field, 1, axis=2))  48.6 us
    slice x29, local copies, waits for them, and re-layouts, neighbours(): west = jnp.where(row_iota == 0, west_edge, jnp.roll(field, 1, axis=1))  42.2 us
    another operation x20, local copies, waits for them, and re-layouts  41.9 us
    slice x21, local copies, waits for them, and re-layouts, neighbours(): north_edge = shifted(field[:, :, :1], 'gy', -1)  32.5 us
  transfers between devices with their start and end apart: 117, of which 8 were waited for; matrix products, arithmetic and copies ran while one was open for 41% of the time, Pallas kernels for 0%

commit v1 on v0

v1 whole, which is shorter than its diff:
```python
import math

import jax
import jax.numpy as jnp
from jax import lax
from jax.experimental import pallas as pl
from jax.experimental.pallas import tpu as pltpu
from jax.sharding import PartitionSpec as P

NSTEP = 10
LSTEP = 4
HALO = NSTEP


def passed_along(value, axis, steps):
    count = lax.axis_size(axis)
    pairs = [(source, (source + steps) % count) for source in range(count)]
    return lax.ppermute(value, axis, pairs)


def shifted(value, axis, steps):
    count = lax.axis_size(axis)
    initial, last = (max(0, -steps), min(count, count - steps))
    return lax.ppermute(value, axis, [(source, source + steps) for source in range(initial, last)])


def round_up(value, unit):
    return (value + unit - 1) // unit * unit


def extended(field, halo):
    planes, rows, columns = field.shape
    total_rows = round_up(rows + 2 * halo, 8)
    total_columns = round_up(columns + 2 * halo, 128)
    east = passed_along(field[:, :halo, :], "gx", -1)
    west = passed_along(field[:, rows - halo :, :], "gx", 1)
    gap = jnp.zeros((planes, total_rows - rows - 2 * halo, columns), field.dtype)
    wide = jnp.concatenate([field, east, gap, west], axis=1)
    north = shifted(wide[:, :, :halo], "gy", -1)
    south = shifted(wide[:, :, columns - halo :], "gy", 1)
    gap = jnp.zeros((planes, total_rows, total_columns - columns - 2 * halo), field.dtype)
    return jnp.concatenate([wide, north, gap, south], axis=2)


def diffuse_call(ext, first, coef, coef_plane, steps, planes, core, base=None):
    _, rows, columns = ext.shape
    core_rows, core_columns = core

    def kernel(*refs):
        if base is None:
            u_ref, c_ref, o_ref = refs
        else:
            u_ref, c_ref, b_ref, o_ref = refs
        c = c_ref[0]
        face_x = c * pltpu.roll(c, rows - 1, 0)
        face_y = c * pltpu.roll(c, columns - 1, 1)

        def step(index, u):
            flux_x = face_x * (pltpu.roll(u, rows - 1, 0) - u)
            change_x = flux_x - pltpu.roll(flux_x, 1, 0)
            flux_y = face_y * (pltpu.roll(u, columns - 1, 1) - u)
            change_y = flux_y - pltpu.roll(flux_y, 1, 1)
            return u + change_x + change_y

        u = lax.fori_loop(0, steps, step, u_ref[0], unroll=True)
        kept = u[:core_rows, :core_columns]
        if base is None:
            o_ref[0] = kept
        else:
            o_ref[0] = b_ref[0] + kept

    in_specs = [
        pl.BlockSpec((1, rows, columns), lambda p: (p + first, 0, 0)),
        pl.BlockSpec((1, rows, columns), coef_plane),
    ]
    operands = [ext, coef]
    if base is not None:
        in_specs.append(pl.BlockSpec((1, core_rows, core_columns), lambda p: (p, 0, 0)))
        operands.append(base)
    return pl.pallas_call(
        kernel,
        grid=(planes,),
        in_specs=in_specs,
        out_specs=pl.BlockSpec((1, core_rows, core_columns), lambda p: (p, 0, 0)),
        out_shape=jax.ShapeDtypeStruct((planes, core_rows, core_columns), jnp.float32),
    )(*operands)


def on_device(
    control, perturb, weights, kappa, wet_levels, obs_index, obs_count, innov, obs_weight
):
    planes, cells_x, cells_y = control.shape
    members = weights.shape[0]
    levels = (planes - 1) // 2
    core = (cells_x, cells_y)
    stack = jnp.concatenate(
        [control, weights, kappa, wet_levels.astype(jnp.float32)[None]], axis=0
    )
    ext = extended(stack, HALO)
    first_kappa = planes + members
    kappa_ext = ext[first_kappa : first_kappa + 4]
    wet_ext = ext[first_kappa + 4]
    level_iota = lax.broadcasted_iota(jnp.int32, (levels, 1, 1), 0).astype(jnp.float32)
    wet_mask = (level_iota < wet_ext[None]).astype(jnp.float32)
    surface = wet_mask[0:1]
    coef = jnp.concatenate(
        [kappa_ext[0:1] * wet_mask, kappa_ext[1:2] * wet_mask, kappa_ext[2:3] * surface, kappa_ext[3:4] * surface],
        axis=0,
    )
    static_plane = lambda p: (p, 0, 0)
    local_plane = lambda p: (planes, 0, 0)
    member_scale = 1.0 / math.sqrt(members * lax.axis_size("ma"))
    static = diffuse_call(ext, 0, coef, static_plane, NSTEP, planes, core)
    local = diffuse_call(ext, planes, coef, local_plane, LSTEP, members, core)
    partial_sum = member_scale * jnp.sum(perturb.astype(jnp.float32) * local[:, None], axis=0)
    ensemble_seen = lax.psum(partial_sum.reshape(-1)[obs_index], "ma")
    static_seen = static.reshape(-1)[obs_index]
    observed = static_seen + ensemble_seen
    live_obs = lax.broadcasted_iota(jnp.int32, obs_index.shape, 0) < obs_count[0]
    misfit = obs_weight * (observed - innov)
    resid = jnp.where(live_obs, misfit, jnp.zeros_like(misfit))
    adjoint = jnp.zeros((planes * cells_x * cells_y,), jnp.float32).at[obs_index].add(resid)
    adjoint = adjoint.reshape(planes, cells_x, cells_y)
    project = member_scale * jnp.sum(perturb.astype(jnp.float32) * adjoint[None], axis=1)
    ext2 = extended(jnp.concatenate([adjoint, project], axis=0), HALO)
    grad_control = diffuse_call(ext2, 0, coef, static_plane, NSTEP, planes, core, base=control)
    grad_weights = diffuse_call(ext2, planes, coef, local_plane, LSTEP, members, core, base=weights)
    return (grad_control, grad_weights)


def solution(mesh):
    placed = (
        P(None, "gx", "gy"),
        P("ma", None, "gx", "gy"),
        P("ma", "gx", "gy"),
        P(None, "gx", "gy"),
        P("gx", "gy"),
        P(("gx", "gy")),
        P(("gx", "gy")),
        P(("gx", "gy")),
        P(("gx", "gy")),
    )
    return jax.shard_map(
        on_device,
        mesh=mesh,
        in_specs=placed,
        out_specs=(P(None, "gx", "gy"), P("ma", "gx", "gy")),
        check_vma=False,
    )
```

time: 858 us -> 251 us (0.29)
  starting transfers between devices: 325 us -> 21.8 us
  local copies, waits for them, and re-layouts: 316 us -> 47 us
  other arithmetic: 177 us -> 23.7 us
  Pallas kernels: 0 us -> 119 us
  between operations: 15 us -> 1.64 us
  waiting for transfers between devices: 16.9 us -> 26.8 us
    ppermute x58 -> x4, starting transfers between devices: 230 us -> 15.1 us  [shifted(): lax.ppermute(value, axis, [(source, source + steps) for source in range(i...]
    slice x162 -> x6, local copies, waits for them, and re-layouts: 179 us -> 11.7 us  [the longest x4 9.13 us: extended(): north = shifted(wide[:, :, :halo], 'gy', -1)]
    add x30 -> x0, other arithmetic: 139 us -> none  [the longest x28 135 us: local_step(): return field + change_x + change_y]
    pallas_call x0 -> x4, Pallas kernels: none -> 119 us  [diffuse_call(): pl.pallas_call(kernel, grid=(planes,), in_specs=in_specs, out_specs=pl.Bl...]
    ppermute x58 -> x4, starting transfers between devices: 94.5 us -> 6.62 us  [passed_along(): return lax.ppermute(value, axis, pairs)]
    another operation x20 -> x0, local copies, waits for them, and re-layouts: 41.9 us -> none
    broadcast_in_dim x58 -> x3, local copies, waits for them, and re-layouts: 17.3 us -> 0.03 us  [the longest x2 0.02 us: extended(): jnp.zeros((planes, total_rows - rows - 2 * halo, columns), field.dtype)]
    gather x1, local copies, waits for them, and re-layouts: 26.3 us -> 11.8 us  [on_device(): static_seen = static.reshape(-1)[obs_index]]
  transfers between devices with their start and end apart: 117 -> 8, of which waited for: 8 -> 5; matrix products, arithmetic and copies ran while one was open for 41% -> 2% of each run, Pallas kernels for 0% -> 0%
where the time goes in v1:
time: 251 us; the launch traced here: 247 us
  Pallas kernels  119 us (47%)
  local copies, waits for them, and re-layouts  47 us (19%)
  waiting for transfers between devices  26.8 us (11%)
  other arithmetic  23.7 us (9%)
  starting transfers between devices  21.8 us (9%)
  blocking collectives  7.28 us (3%)
    pallas_call x4, Pallas kernels, diffuse_call(): pl.pallas_call(kernel, grid=(planes,), in_specs=in_specs, out_specs=pl.Bl...  119 us
    ppermute x4, starting transfers between devices, shifted(): lax.ppermute(value, axis, [(source, source + steps) for source in range(i...  15.1 us
    ppermute x4, waiting for transfers between devices, passed_along(): return lax.ppermute(value, axis, pairs)  14.7 us
    ppermute x4, waiting for transfers between devices, shifted(): lax.ppermute(value, axis, [(source, source + steps) for source in range(i...  12.2 us
    gather x1, local copies, waits for them, and re-layouts, on_device(): ensemble_seen = lax.psum(partial_sum.reshape(-1)[obs_index], 'ma')  11.8 us
    gather x1, local copies, waits for them, and re-layouts, on_device(): static_seen = static.reshape(-1)[obs_index]  11.8 us
    scatter-add x1, other arithmetic, on_device(): jnp.zeros((planes * cells_x * cells_y,), jnp.float32).at[obs_index]  11.5 us
    slice x4, local copies, waits for them, and re-layouts, extended(): north = shifted(wide[:, :, :halo], 'gy', -1)  9.13 us
  transfers between devices with their start and end apart: 8, of which 5 were waited for; matrix products, arithmetic and copies ran while one was open for 2% of the time, Pallas kernels for 0%

profile of v1, /device:TPU:126, one launch (start us, length us, event | category | flops | bytes accessed | tf_op | source)
XLA Modules:
  0.0 247.1 jit_solution(6027948542997863830)
XLA Ops:
  3.5 2.5 %collective-permute-start.1 = (f32[42,10,128]{2,1,0:T(8,128)S(1)}, f32[42,10,128]{2,1,0:T(8,128)S(1)}, u32[]{:S(2)}, u32[]{:S(2)}) collective-permute-start(f32[42,10,128]{2,1,0:T(8,128)S(1)} %get-tuple-element.11), channel_id=1, source_target_pairs={{0,64},{64,128},{128,192},{192,0},{1,65},{65,129},{129,193},{193,1... | collective-permute-start | bytes 645128 | tf_op jit(solution)/shard_map/ppermute | solution.py:18
  6.0 7.8 %collective-permute-done = f32[42,10,128]{2,1,0:T(8,128)S(1)} collective-permute-done((f32[42,10,128]{2,1,0:T(8,128)S(1)}, f32[42,10,128]{2,1,0:T(8,128)S(1)}, u32[]{:S(2)}, u32[]{:S(2)}) %collective-permute-start) | collective-permute-done | bytes 215072 | tf_op jit(solution)/shard_map/ppermute | solution.py:18
  14.6 1.9 fusion.4
  16.5 2.9 %copy.11 = f32[42,88,10]{1,0,2:T(8,128)} copy(f32[42,88,10]{2,1,0:T(8,128)} %get-tuple-element.6) | data formatting | bytes 295680 | tf_op jit(solution)/shard_map/slice | solution.py:39
  19.4 1.4 copy.12
  20.7 5.3 %collective-permute-start.3 = (f32[42,88,10]{1,0,2:T(8,128)}, f32[42,88,10]{1,0,2:T(8,128)}, u32[]{:S(2)}, u32[]{:S(2)}) collective-permute-start(f32[42,88,10]{1,0,2:T(8,128)} %copy.12), channel_id=1, source_target_pairs={{0,4},{4,8},{8,12},{12,16},{16,20},{20,24},{24,28},{28,32},{32,36}... | collective-permute-start | bytes 443528 | tf_op jit(solution)/shard_map/ppermute | solution.py:24
  26.0 1.9 collective-permute-start.2
  28.7 8.2 %collective-permute-done.2 = f32[42,88,10]{1,0,2:T(8,128)} collective-permute-done((f32[42,88,10]{1,0,2:T(8,128)}, f32[42,88,10]{1,0,2:T(8,128)}, u32[]{:S(2)}, u32[]{:S(2)}) %collective-permute-start.2) | collective-permute-done | bytes 147872 | tf_op jit(solution)/shard_map/ppermute | solution.py:24
  36.9 1.5 copy.13
  38.5 2.8 %copy.14 = f32[42,88,10]{2,1,0:T(8,128)} copy(f32[42,88,10]{1,0,2:T(8,128)} %collective-permute-done.3) | data formatting | bytes 295680 | tf_op jit(solution)/shard_map/ppermute | solution.py:24
  41.3 2.8 %pad_maximum_fusion.refs_0_ = f32[42,88,256]{2,1,0:T(8,128)S(1)} fusion(f32[42,88,10]{2,1,0:T(8,128)} %copy.14, f32[42,88,10]{2,1,0:T(8,128)S(1)} %copy.13, f32[42,10,128]{2,1,0:T(8,128)} %copy-done.7, f32[42,4,128]{2,1,0:T(4,128)S(1)} %broadcast_in_dim.30, f32[42,10,128]{2,1,0:T(8,128)} %copy-done.6, f32[1,64,128]{2,1,0:T(8,128)S(1)} %convert_bitcast_fusion, ...), kind=kLoop, calls=%fused_computation.7 | loop fusion | flops 8515584 | bytes 5973760 | tf_op jit(solution)/shard_map/concatenate | solution.py:42
  44.8 1.3 copy-done.1
  46.1 1.8 pad_maximum_fusion.2.refs_1_
  47.9 4.4 %shard_map.105 = f32[4,64,128]{2,1,0:T(8,128)} custom-call(f32[42,88,256]{2,1,0:T(8,128)} %copy-done.1, f32[34,88,256]{2,1,0:T(8,128)} %pad_maximum_fusion.2.refs_1_), custom_call_target="tpu_custom_call" | custom-call | tf_op jit(solution)/shard_map/pallas_call | solution.py:80
  52.3 55.0 %shard_map.104 = f32[33,64,128]{2,1,0:T(8,128)} custom-call(f32[42,88,256]{2,1,0:T(8,128)} %copy-done.1, f32[34,88,256]{2,1,0:T(8,128)} %pad_maximum_fusion.2.refs_1_), custom_call_target="tpu_custom_call" | custom-call | tf_op jit(solution)/shard_map/pallas_call | solution.py:80
  109.0 11.8 %gather_fusion = f32[2048]{0:T(1024)S(1)} fusion(f32[270336]{0:T(1024)S(1)} %bitcast.14, s32[2048]{0:T(1024)S(1)} %get-tuple-element.16), kind=kCustom, calls=%fused_computation | custom fusion | bytes 24576 | tf_op jit(solution)/shard_map/gather | solution.py:117
  120.8 11.8 %gather_fusion.1 = f32[2048]{0:T(1024)S(1)} fusion(f32[270336]{0:T(1024)S(1)} %bitcast.13, s32[2048]{0:T(1024)S(1)} %get-tuple-element.16), kind=kCustom, calls=%fused_computation.1 | custom fusion | bytes 24576 | tf_op jit(solution)/shard_map/gather | solution.py:116
  132.6 7.3 %psum.7 = f32[2048]{0:T(1024)S(1)} all-reduce(f32[2048]{0:T(1024)S(1)} %gather_fusion.1), channel_id=1, replica_groups=mesh['gx'=4,'gy'=16,'ma'=4] {'ma'}, use_global_device_ids=true, to_apply=%region_1.0 | all-reduce | flops 2048 | bytes 16384 | tf_op jit(solution)/shard_map/psum | solution.py:116
  140.0 11.5 %scatter_custom_fusion = f32[270336]{0:T(1024)S(1)} fusion(s32[2048]{0:T(1024)S(1)} %get-tuple-element.17, f32[2048]{0:T(1024)S(1)} %multiply_select_fusion, f32[]{:T(128)} %constant.4.clone.1), kind=kCustom, calls=%fused_computation.16 | custom fusion | flops 2048 | bytes 1081348 | tf_op jit(solution)/shard_map/scatter-add | solution.py:122
  152.1 3.2 %collective-permute-start.5 = (f32[37,10,128]{2,1,0:T(8,128)S(1)}, f32[37,10,128]{2,1,0:T(8,128)S(1)}, u32[]{:S(2)}, u32[]{:S(2)}) collective-permute-start(f32[37,10,128]{2,1,0:T(8,128)S(1)} %get-tuple-element.13), channel_id=1, source_target_pairs={{0,64},{64,128},{128,192},{192,0},{1,65},{65,129},{129,193},{193,1... | collective-permute-start | bytes 568328 | tf_op jit(solution)/shard_map/ppermute | solution.py:18
  155.4 6.9 %collective-permute-done.4 = f32[37,10,128]{2,1,0:T(8,128)S(1)} collective-permute-done((f32[37,10,128]{2,1,0:T(8,128)S(1)}, f32[37,10,128]{2,1,0:T(8,128)S(1)}, u32[]{:S(2)}, u32[]{:S(2)}) %collective-permute-start.4) | collective-permute-done | bytes 189472 | tf_op jit(solution)/shard_map/ppermute | solution.py:18
  162.5 1.7 fusion.5
  164.2 2.7 %copy.15 = f32[37,88,10]{1,0,2:T(8,128)} copy(f32[37,88,10]{2,1,0:T(8,128)} %get-tuple-element.8) | data formatting | bytes 260480 | tf_op jit(solution)/shard_map/slice | solution.py:39
  166.9 1.9 collective-permute-start.6
  168.8 1.2 copy.16
  170.0 6.0 %collective-permute-start.7 = (f32[37,88,10]{1,0,2:T(8,128)}, f32[37,88,10]{1,0,2:T(8,128)}, u32[]{:S(2)}, u32[]{:S(2)}) collective-permute-start(f32[37,88,10]{1,0,2:T(8,128)} %copy.16), channel_id=1, source_target_pairs={{0,4},{4,8},{8,12},{12,16},{16,20},{20,24},{24,28},{28,32},{32,36}... | collective-permute-start | bytes 390728 | tf_op jit(solution)/shard_map/ppermute | solution.py:24
  177.2 1.5 copy.17
  178.7 2.8 %collective-permute-done.7 = f32[37,88,10]{1,0,2:T(8,128)} collective-permute-done((f32[37,88,10]{1,0,2:T(8,128)}, f32[37,88,10]{1,0,2:T(8,128)}, u32[]{:S(2)}, u32[]{:S(2)}) %collective-permute-start.7) | collective-permute-done | bytes 130272 | tf_op jit(solution)/shard_map/ppermute | solution.py:24
  181.5 2.7 %copy.18 = f32[37,88,10]{2,1,0:T(8,128)} copy(f32[37,88,10]{1,0,2:T(8,128)} %collective-permute-done.7) | data formatting | bytes 260480 | tf_op jit(solution)/shard_map/ppermute | solution.py:24
  184.2 3.5 %pad_maximum_fusion.1.refs_0_ = f32[37,88,256]{2,1,0:T(8,128)} fusion(f32[37,88,10]{2,1,0:T(8,128)} %copy.18, f32[37,88,10]{2,1,0:T(8,128)S(1)} %copy.17, f32[37,10,128]{2,1,0:T(8,128)S(1)} %collective-permute-done.5, f32[37,4,128]{2,1,0:T(4,128)} %copy-done.9, f32[37,10,128]{2,1,0:T(8,128)S(1)} %collective-permute-done.4, ...), kind=kLoop, calls=%fused_computation.8 | loop fusion | flops 5834752 | bytes 5262720 | tf_op jit(solution)/shard_map/concatenate | solution.py:42
  187.7 4.5 %shard_map.107 = f32[4,64,128]{2,1,0:T(8,128)} custom-call(f32[37,88,256]{2,1,0:T(8,128)} %pad_maximum_fusion.1.refs_0_, f32[34,88,256]{2,1,0:T(8,128)} %pad_maximum_fusion.2.refs_1_, f32[4,64,128]{2,1,0:T(8,128)} %refs_2_.3), custom_call_target="tpu_custom_call" | custom-call | tf_op jit(solution)/shard_map/pallas_call | solution.py:80
  192.2 55.0 %shard_map.106 = f32[33,64,128]{2,1,0:T(8,128)} custom-call(f32[37,88,256]{2,1,0:T(8,128)} %pad_maximum_fusion.1.refs_0_, f32[34,88,256]{2,1,0:T(8,128)} %pad_maximum_fusion.2.refs_1_, f32[33,64,128]{2,1,0:T(8,128)} %refs_2_.2), custom_call_target="tpu_custom_call" | custom-call | tf_op jit(solution)/shard_map/pallas_call | solution.py:80
  (53 shorter events, 8.0 us)
Async XLA Ops:
  0.6 13.2 %copy-start.5 = (f32[4,64,128]{2,1,0:T(8,128)S(1)}, f32[4,64,128]{2,1,0:T(8,128)}, u32[]{:S(2)}) copy-start(f32[4,64,128]{2,1,0:T(8,128)} %refs_2_.3) | copy-start | bytes 393220
  0.6 13.2 %copy-start.2 = (f32[33,64,128]{2,1,0:T(8,128)S(1)}, f32[33,64,128]{2,1,0:T(8,128)}, u32[]{:S(2)}) copy-start(f32[33,64,128]{2,1,0:T(8,128)} %refs_2_.2) | copy-start | bytes 3244036
  0.7 13.2 %copy-start.8 = (f32[4,64,128]{2,1,0:T(8,128)S(1)}, f32[4,64,128]{2,1,0:T(8,128)}, u32[]{:S(2)}) copy-start(f32[4,64,128]{2,1,0:T(8,128)} %param.12) | copy-start | bytes 393220
  2.7 11.1 %collective-permute-start = (f32[42,10,128]{2,1,0:T(8,128)S(1)}, f32[42,10,128]{2,1,0:T(8,128)S(1)}, u32[]{:S(2)}, u32[]{:S(2)}) collective-permute-start(f32[42,10,128]{2,1,0:T(8,128)S(1)} %get-tuple-element.10), channel_id=1, source_target_pairs={{0,192},{64,0},{128,64},{192,128},{1,193},{65,1},{129,65},{193,129... | collective-permute-start | bytes 645128 | tf_op jit(solution)/shard_map/ppermute | solution.py:18
  3.5 10.3 %collective-permute-start.1 = (f32[42,10,128]{2,1,0:T(8,128)S(1)}, f32[42,10,128]{2,1,0:T(8,128)S(1)}, u32[]{:S(2)}, u32[]{:S(2)}) collective-permute-start(f32[42,10,128]{2,1,0:T(8,128)S(1)} %get-tuple-element.11), channel_id=1, source_target_pairs={{0,64},{64,128},{128,192},{192,0},{1,65},{65,129},{129,193},{193,1... | collective-permute-start | bytes 645128 | tf_op jit(solution)/shard_map/ppermute | solution.py:18
  13.8 0.7 copy-start.6
  13.8 0.8 copy-start.7
  16.5 11.5 %copy-start.11 = (s32[2048]{0:T(1024)S(1)}, s32[2048]{0:T(1024)}, u32[]{:S(2)}) copy-start(s32[2048]{0:T(1024)} %param.14) | copy-start | bytes 24580
  20.7 17.7 %collective-permute-start.3 = (f32[42,88,10]{1,0,2:T(8,128)}, f32[42,88,10]{1,0,2:T(8,128)}, u32[]{:S(2)}, u32[]{:S(2)}) collective-permute-start(f32[42,88,10]{1,0,2:T(8,128)} %copy.12), channel_id=1, source_target_pairs={{0,4},{4,8},{8,12},{12,16},{16,20},{20,24},{24,28},{28,32},{32,36}... | collective-permute-start | bytes 443528 | tf_op jit(solution)/shard_map/ppermute | solution.py:24
  26.0 10.9 %collective-permute-start.2 = (f32[42,88,10]{1,0,2:T(8,128)}, f32[42,88,10]{1,0,2:T(8,128)}, u32[]{:S(2)}, u32[]{:S(2)}) collective-permute-start(f32[42,88,10]{1,0,2:T(8,128)} %copy.11), channel_id=1, source_target_pairs={{4,0},{8,4},{12,8},{16,12},{20,16},{24,20},{28,24},{32,28},{36,32}... | collective-permute-start | bytes 443528 | tf_op jit(solution)/shard_map/ppermute | solution.py:24
  44.2 1.9 copy-start.1
  52.3 55.0 %copy-start.3 = (bf16[4,33,64,128]{3,2,1,0:T(8,128)(2,1)S(1)}, bf16[4,33,64,128]{3,2,1,0:T(8,128)(2,1)}, u32[]{:S(2)}) copy-start(bf16[4,33,64,128]{3,2,1,0:T(8,128)(2,1)} %param.10) | copy-start | bytes 6488068
  52.3 55.0 %copy-start.10 = (f32[4,64,128]{2,1,0:T(8,128)S(1)}, f32[4,64,128]{2,1,0:T(8,128)}, u32[]{:S(2)}) copy-start(f32[4,64,128]{2,1,0:T(8,128)} %shard_map.105) | copy-start | bytes 393220
  107.8 1.2 copy-start
  120.8 19.1 %copy-start.12 = (f32[2048]{0:T(1024)S(1)}, f32[2048]{0:T(1024)}, u32[]{:S(2)}) copy-start(f32[2048]{0:T(1024)} %param.17) | copy-start | bytes 24580
  120.8 19.1 %copy-start.13 = (f32[2048]{0:T(1024)S(1)}, f32[2048]{0:T(1024)}, u32[]{:S(2)}) copy-start(f32[2048]{0:T(1024)} %param.16) | copy-start | bytes 24580
  120.8 30.7 %copy-start.4 = (bf16[4,33,64,128]{3,2,1,0:T(8,128)(2,1)S(1)}, bf16[4,33,64,128]{3,2,1,0:T(8,128)(2,1)}, u32[]{:S(2)}) copy-start(bf16[4,33,64,128]{3,2,1,0:T(8,128)(2,1)} %param.10) | copy-start | bytes 6488068
  152.0 10.2 %collective-permute-start.4 = (f32[37,10,128]{2,1,0:T(8,128)S(1)}, f32[37,10,128]{2,1,0:T(8,128)S(1)}, u32[]{:S(2)}, u32[]{:S(2)}) collective-permute-start(f32[37,10,128]{2,1,0:T(8,128)S(1)} %get-tuple-element.12), channel_id=1, source_target_pairs={{0,192},{64,0},{128,64},{192,128},{1,193},{65,1},{129,65},{193,129... | collective-permute-start | bytes 568328 | tf_op jit(solution)/shard_map/ppermute | solution.py:18
  152.1 10.1 %collective-permute-start.5 = (f32[37,10,128]{2,1,0:T(8,128)S(1)}, f32[37,10,128]{2,1,0:T(8,128)S(1)}, u32[]{:S(2)}, u32[]{:S(2)}) collective-permute-start(f32[37,10,128]{2,1,0:T(8,128)S(1)} %get-tuple-element.13), channel_id=1, source_target_pairs={{0,64},{64,128},{128,192},{192,0},{1,65},{65,129},{129,193},{193,1... | collective-permute-start | bytes 568328 | tf_op jit(solution)/shard_map/ppermute | solution.py:18
  162.3 1.9 copy-start.9
  166.9 10.4 %collective-permute-start.6 = (f32[37,88,10]{1,0,2:T(8,128)}, f32[37,88,10]{1,0,2:T(8,128)}, u32[]{:S(2)}, u32[]{:S(2)}) collective-permute-start(f32[37,88,10]{1,0,2:T(8,128)} %copy.15), channel_id=1, source_target_pairs={{4,0},{8,4},{12,8},{16,12},{20,16},{24,20},{28,24},{32,28},{36,32}... | collective-permute-start | bytes 390728 | tf_op jit(solution)/shard_map/ppermute | solution.py:24
  170.0 11.5 %collective-permute-start.7 = (f32[37,88,10]{1,0,2:T(8,128)}, f32[37,88,10]{1,0,2:T(8,128)}, u32[]{:S(2)}, u32[]{:S(2)}) collective-permute-start(f32[37,88,10]{1,0,2:T(8,128)} %copy.16), channel_id=1, source_target_pairs={{0,4},{4,8},{8,12},{12,16},{16,20},{20,24},{24,28},{28,32},{32,36}... | collective-permute-start | bytes 390728 | tf_op jit(solution)/shard_map/ppermute | solution.py:24

commit v2 on v1

--- a/solution.py
+++ b/solution.py
@@ -28,18 +28,44 @@
     return (value + unit - 1) // unit * unit
 
 
+def received(value, along_x, along_y):
+    count_x = lax.axis_size("gx")
+    count_y = lax.axis_size("gy")
+    pairs = []
+    for source_x in range(count_x):
+        for source_y in range(count_y):
+            target_y = source_y - along_y
+            if 0 <= target_y < count_y:
+                target_x = (source_x - along_x) % count_x
+                pairs.append((source_x * count_y + source_y, target_x * count_y + target_y))
+    return lax.ppermute(value, ("gx", "gy"), pairs)
+
+
 def extended(field, halo):
     planes, rows, columns = field.shape
     total_rows = round_up(rows + 2 * halo, 8)
     total_columns = round_up(columns + 2 * halo, 128)
-    east = passed_along(field[:, :halo, :], "gx", -1)
-    west = passed_along(field[:, rows - halo :, :], "gx", 1)
-    gap = jnp.zeros((planes, total_rows - rows - 2 * halo, columns), field.dtype)
-    wide = jnp.concatenate([field, east, gap, west], axis=1)
-    north = shifted(wide[:, :, :halo], "gy", -1)
-    south = shifted(wide[:, :, columns - halo :], "gy", 1)
+    first_rows = field[:, :halo]
+    last_rows = field[:, rows - halo :]
+    east = received(first_rows, 1, 0)
+    west = received(last_rows, -1, 0)
+    north = received(field[:, :, :halo], 0, 1)
+    south = received(field[:, :, columns - halo :], 0, -1)
+    east_north = received(first_rows[:, :, :halo], 1, 1)
+    east_south = received(first_rows[:, :, columns - halo :], 1, -1)
+    west_north = received(last_rows[:, :, :halo], -1, 1)
+    west_south = received(last_rows[:, :, columns - halo :], -1, -1)
+
+    def column(middle, after, before):
+        width = middle.shape[2]
+        gap = jnp.zeros((planes, total_rows - rows - 2 * halo, width), field.dtype)
+        return jnp.concatenate([middle, after, gap, before], axis=1)
+
     gap = jnp.zeros((planes, total_rows, total_columns - columns - 2 * halo), field.dtype)
-    return jnp.concatenate([wide, north, gap, south], axis=2)
+    return jnp.concatenate(
+        [column(field, east, west), column(north, east_north, west_north), gap, column(south, east_south, west_south)],
+        axis=2,
+    )
 
 
 def diffuse_call(ext, first, coef, coef_plane, steps, planes, core, base=None):

time: 251 us -> 287 us (1.14)
  starting transfers between devices: 21.8 us -> 53.7 us
  waiting for transfers between devices: 26.8 us -> 35.9 us
  local copies, waits for them, and re-layouts: 47 us -> 38 us
  other arithmetic: 23.7 us -> 28.4 us
    ppermute x8 -> x16, starting transfers between devices: 21.8 us -> 53.7 us  [received(): return lax.ppermute(value, ('gx', 'gy'), pairs)]
    ppermute x8 -> x16, waiting for transfers between devices: 26.8 us -> 35.9 us  [received(): return lax.ppermute(value, ('gx', 'gy'), pairs)]
    concatenate x4 -> x6, other arithmetic: 6.73 us -> 12.7 us  [the longest x2 8.8 us: extended(): jnp.concatenate([column(field, east, west), column(north, east_north, wes...]
    slice x6 -> x7, local copies, waits for them, and re-layouts: 11.7 us -> 6 us  [the longest x3 2.11 us: extended(): north = received(field[:, :, :halo], 0, 1)]
  transfers between devices with their start and end apart: 8 -> 16, of which waited for: 5 -> 8; matrix products, arithmetic and copies ran while one was open for 2% -> 4% of each run, Pallas kernels for 0% -> 0%
where the time goes in v2:
time: 287 us; the launch traced here: 285 us
  Pallas kernels  119 us (41%)
  starting transfers between devices  53.7 us (19%)
  local copies, waits for them, and re-layouts  38 us (13%)
  waiting for transfers between devices  35.9 us (13%)
  other arithmetic  28.4 us (10%)
  blocking collectives  8.09 us (3%)
    pallas_call x4, Pallas kernels, diffuse_call(): pl.pallas_call(kernel, grid=(planes,), in_specs=in_specs, out_specs=pl.Bl...  119 us
    ppermute x16, starting transfers between devices, received(): return lax.ppermute(value, ('gx', 'gy'), pairs)  53.7 us
    ppermute x16, waiting for transfers between devices, received(): return lax.ppermute(value, ('gx', 'gy'), pairs)  35.9 us
    gather x1, local copies, waits for them, and re-layouts, on_device(): ensemble_seen = lax.psum(partial_sum.reshape(-1)[obs_index], 'ma')  11.8 us
    gather x1, local copies, waits for them, and re-layouts, on_device(): static_seen = static.reshape(-1)[obs_index]  11.8 us
    scatter-add x1, other arithmetic, on_device(): jnp.zeros((planes * cells_x * cells_y,), jnp.float32).at[obs_index]  11.5 us
    concatenate x2, other arithmetic, extended(): jnp.concatenate([column(field, east, west), column(north, east_north, wes...  8.8 us
    psum x1, blocking collectives, on_device(): ensemble_seen = lax.psum(partial_sum.reshape(-1)[obs_index], 'ma')  8.09 us
  transfers between devices with their start and end apart: 16, of which 8 were waited for; matrix products, arithmetic and copies ran while one was open for 4% of the time, Pallas kernels for 0%

profile of v2, /device:TPU:126, one launch (start us, length us, event | category | flops | bytes accessed | tf_op | source)
XLA Modules:
  0.0 284.8 jit_solution(1452026150370026498)
XLA Ops:
  4.5 2.5 collective-permute-start.1
  8.3 1.9 collective-permute-start.3
  11.9 5.3 %collective-permute-start.5 = (f32[42,64,10]{1,0,2:T(8,128)}, f32[42,64,10]{1,0,2:T(8,128)S(1)}, u32[]{:S(2)}, u32[]{:S(2)}) collective-permute-start(f32[42,64,10]{1,0,2:T(8,128)} %copy.29), channel_id=1, source_target_pairs={{0,4},{4,8},{8,12},{12,16},{16,20},{20,24},{24,28},{28,32},{32,36}... | collective-permute-start | bytes 322568 | tf_op jit(solution)/shard_map/ppermute | solution.py:41
  17.8 1.9 collective-permute-start.2
  19.7 4.5 %collective-permute-done.3 = f32[42,10,10]{2,1,0:T(8,128)} collective-permute-done((f32[42,10,10]{2,1,0:T(8,128)}, f32[42,10,10]{2,1,0:T(8,128)}, u32[]{:S(2)}, u32[]{:S(2)}) %collective-permute-start.3) | collective-permute-done | bytes 16832 | tf_op jit(solution)/shard_map/ppermute | solution.py:41
  24.2 7.5 %collective-permute-start.6 = (f32[42,10,10]{2,1,0:T(8,128)}, f32[42,10,10]{2,1,0:T(8,128)}, u32[]{:S(2)}, u32[]{:S(2)}) collective-permute-start(f32[42,10,10]{2,1,0:T(8,128)} %get-tuple-element.11), channel_id=1, source_target_pairs={{0,196},{4,200},{8,204},{12,208},{16,212},{20,216},{24,220},{28,22... | collective-permute-start | bytes 50408 | tf_op jit(solution)/shard_map/ppermute | solution.py:41
  31.9 4.1 %collective-permute-start.4 = (f32[42,10,10]{2,1,0:T(8,128)}, f32[42,10,10]{2,1,0:T(8,128)}, u32[]{:S(2)}, u32[]{:S(2)}) collective-permute-start(f32[42,10,10]{2,1,0:T(8,128)} %get-tuple-element.12), channel_id=1, source_target_pairs={{4,64},{8,68},{12,72},{16,76},{20,80},{24,84},{28,88},{32,92},{36,... | collective-permute-start | bytes 50408 | tf_op jit(solution)/shard_map/ppermute | solution.py:41
  36.1 5.2 %collective-permute-start.7 = (f32[42,10,10]{2,1,0:T(8,128)}, f32[42,10,10]{2,1,0:T(8,128)}, u32[]{:S(2)}, u32[]{:S(2)}) collective-permute-start(f32[42,10,10]{2,1,0:T(8,128)} %get-tuple-element.13), channel_id=1, source_target_pairs={{0,68},{4,72},{8,76},{12,80},{16,84},{20,88},{24,92},{28,96},{32,1... | collective-permute-start | bytes 50408 | tf_op jit(solution)/shard_map/ppermute | solution.py:41
  43.7 2.5 copy.30
  46.2 3.1 %collective-permute-done.6 = f32[42,10,10]{2,1,0:T(8,128)} collective-permute-done((f32[42,10,10]{2,1,0:T(8,128)}, f32[42,10,10]{2,1,0:T(8,128)}, u32[]{:S(2)}, u32[]{:S(2)}) %collective-permute-start.6) | collective-permute-done | bytes 16832 | tf_op jit(solution)/shard_map/ppermute | solution.py:41
  51.1 3.3 %collective-permute-done.7 = f32[42,10,10]{2,1,0:T(8,128)} collective-permute-done((f32[42,10,10]{2,1,0:T(8,128)}, f32[42,10,10]{2,1,0:T(8,128)}, u32[]{:S(2)}, u32[]{:S(2)}) %collective-permute-start.7) | collective-permute-done | bytes 16832 | tf_op jit(solution)/shard_map/ppermute | solution.py:41
  54.5 4.1 %maximum_maximum_fusion.refs_0_ = f32[42,88,256]{2,1,0:T(8,128)S(1)} fusion(f32[42,10,10]{2,1,0:T(8,128)} %collective-permute-done.7, f32[42,4,10]{2,1,0:T(4,128)S(1)} %broadcast.26, f32[42,10,10]{2,1,0:T(8,128)} %collective-permute-done.6, f32[42,64,10]{2,1,0:T(8,128)} %copy.30, f32[42,10,10]{2,1,0:T(8,128)} %collective-permute-done.4, ...), kind=kLoop, calls=%fused_computation.14 | loop fusion | flops 14192640 | bytes 5971136 | tf_op jit(solution)/shard_map/concatenate | solution.py:65
  60.4 1.9 pad_maximum_fusion.refs_1_
  62.3 4.4 %shard_map.105 = f32[4,64,128]{2,1,0:T(8,128)} custom-call(f32[42,88,256]{2,1,0:T(8,128)} %copy-done.1, f32[34,88,256]{2,1,0:T(8,128)} %pad_maximum_fusion.refs_1_), custom_call_target="tpu_custom_call" | custom-call | tf_op jit(solution)/shard_map/pallas_call | solution.py:106
  66.8 55.0 %shard_map.104 = f32[33,64,128]{2,1,0:T(8,128)} custom-call(f32[42,88,256]{2,1,0:T(8,128)} %copy-done.1, f32[34,88,256]{2,1,0:T(8,128)} %pad_maximum_fusion.refs_1_), custom_call_target="tpu_custom_call" | custom-call | tf_op jit(solution)/shard_map/pallas_call | solution.py:106
  123.5 11.8 %gather_fusion = f32[2048]{0:T(1024)S(1)} fusion(f32[270336]{0:T(1024)S(1)} %bitcast.14, s32[2048]{0:T(1024)S(1)} %get-tuple-element.24), kind=kCustom, calls=%fused_computation | custom fusion | bytes 24576 | tf_op jit(solution)/shard_map/gather | solution.py:143
  135.3 11.8 %gather_fusion.1 = f32[2048]{0:T(1024)S(1)} fusion(f32[270336]{0:T(1024)S(1)} %bitcast.13, s32[2048]{0:T(1024)S(1)} %get-tuple-element.24), kind=kCustom, calls=%fused_computation.1 | custom fusion | bytes 24576 | tf_op jit(solution)/shard_map/gather | solution.py:142
  147.1 8.1 %psum.7 = f32[2048]{0:T(1024)S(1)} all-reduce(f32[2048]{0:T(1024)S(1)} %gather_fusion.1), channel_id=1, replica_groups=mesh['gx'=4,'gy'=16,'ma'=4] {'ma'}, use_global_device_ids=true, to_apply=%region_1.0 | all-reduce | flops 2048 | bytes 16384 | tf_op jit(solution)/shard_map/psum | solution.py:142
  155.2 11.5 %scatter_custom_fusion = f32[270336]{0:T(1024)S(1)} fusion(s32[2048]{0:T(1024)S(1)} %get-tuple-element.25, f32[2048]{0:T(1024)S(1)} %multiply_select_fusion, f32[]{:T(128)} %constant.4.clone.1), kind=kCustom, calls=%fused_computation.29 | custom fusion | flops 2048 | bytes 1081348 | tf_op jit(solution)/shard_map/scatter-add | solution.py:148
  168.6 4.2 %collective-permute-start.9 = (f32[37,10,128]{2,1,0:T(8,128)}, f32[37,10,128]{2,1,0:T(8,128)}, u32[]{:S(2)}, u32[]{:S(2)}) collective-permute-start(f32[37,10,128]{2,1,0:T(8,128)} %get-tuple-element.15), channel_id=1, source_target_pairs={{0,64},{4,68},{8,72},{12,76},{16,80},{20,84},{24,88},{28,92},{32,9... | collective-permute-start | bytes 568328 | tf_op jit(solution)/shard_map/ppermute | solution.py:41
  174.7 1.9 collective-permute-start.13
  176.7 3.9 %collective-permute-start.10 = (f32[37,64,10]{1,0,2:T(8,128)}, f32[37,64,10]{1,0,2:T(8,128)S(1)}, u32[]{:S(2)}, u32[]{:S(2)}) collective-permute-start(f32[37,64,10]{1,0,2:T(8,128)} %copy.31), channel_id=1, source_target_pairs={{4,0},{8,4},{12,8},{16,12},{20,16},{24,20},{28,24},{32,28},{36,32}... | collective-permute-start | bytes 284168 | tf_op jit(solution)/shard_map/ppermute | solution.py:41
  181.7 1.9 collective-permute-start.11
  183.6 11.2 %collective-permute-done.11 = f32[37,10,10]{2,1,0:T(8,128)S(1)} collective-permute-done((f32[37,10,10]{2,1,0:T(8,128)S(1)}, f32[37,10,10]{2,1,0:T(8,128)S(1)}, u32[]{:S(2)}, u32[]{:S(2)}) %collective-permute-start.11) | collective-permute-done | bytes 14832 | tf_op jit(solution)/shard_map/ppermute | solution.py:41
  194.8 1.9 collective-permute-start.12
  196.8 6.7 %collective-permute-start.15 = (f32[37,10,10]{2,1,0:T(8,128)}, f32[37,10,10]{2,1,0:T(8,128)}, u32[]{:S(2)}, u32[]{:S(2)}) collective-permute-start(f32[37,10,10]{2,1,0:T(8,128)} %get-tuple-element.20), channel_id=1, source_target_pairs={{0,68},{4,72},{8,76},{12,80},{16,84},{20,88},{24,92},{28,96},{32,1... | collective-permute-start | bytes 44408 | tf_op jit(solution)/shard_map/ppermute | solution.py:41
  203.5 3.5 %collective-permute-start.14 = (f32[37,10,10]{2,1,0:T(8,128)}, f32[37,10,10]{2,1,0:T(8,128)}, u32[]{:S(2)}, u32[]{:S(2)}) collective-permute-start(f32[37,10,10]{2,1,0:T(8,128)} %get-tuple-element.21), channel_id=1, source_target_pairs={{0,196},{4,200},{8,204},{12,208},{16,212},{20,216},{24,220},{28,22... | collective-permute-start | bytes 44408 | tf_op jit(solution)/shard_map/ppermute | solution.py:41
  208.8 6.2 %collective-permute-done.12 = f32[37,10,10]{2,1,0:T(8,128)} collective-permute-done((f32[37,10,10]{2,1,0:T(8,128)}, f32[37,10,10]{2,1,0:T(8,128)}, u32[]{:S(2)}, u32[]{:S(2)}) %collective-permute-start.12) | collective-permute-done | bytes 14832 | tf_op jit(solution)/shard_map/ppermute | solution.py:41
  215.0 5.6 %collective-permute-done.14 = f32[37,10,10]{2,1,0:T(8,128)} collective-permute-done((f32[37,10,10]{2,1,0:T(8,128)}, f32[37,10,10]{2,1,0:T(8,128)}, u32[]{:S(2)}, u32[]{:S(2)}) %collective-permute-start.14) | collective-permute-done | bytes 14832 | tf_op jit(solution)/shard_map/ppermute | solution.py:41
  220.6 4.7 %maximum_maximum_fusion.1.refs_0_ = f32[37,88,256]{2,1,0:T(8,128)} fusion(f32[37,10,10]{2,1,0:T(8,128)} %collective-permute-done.15, f32[37,4,10]{2,1,0:T(4,128)S(1)} %broadcast.29, f32[37,10,10]{2,1,0:T(8,128)} %collective-permute-done.14, f32[37,64,10]{2,1,0:T(8,128)S(1)} %copy.34, f32[37,10,10]{2,1,0:T(8,128)} %collective-permute-done.12, ...), kind=kLoop, calls=%fused_computation.15 | loop fusion | flops 10835968 | bytes 5271136 | tf_op jit(solution)/shard_map/concatenate | solution.py:65
  225.3 4.5 %shard_map.107 = f32[4,64,128]{2,1,0:T(8,128)} custom-call(f32[37,88,256]{2,1,0:T(8,128)} %maximum_maximum_fusion.1.refs_0_, f32[34,88,256]{2,1,0:T(8,128)} %pad_maximum_fusion.refs_1_, f32[4,64,128]{2,1,0:T(8,128)} %refs_2_.3), custom_call_target="tpu_custom_call" | custom-call | tf_op jit(solution)/shard_map/pallas_call | solution.py:106
  229.8 55.0 %shard_map.106 = f32[33,64,128]{2,1,0:T(8,128)} custom-call(f32[37,88,256]{2,1,0:T(8,128)} %maximum_maximum_fusion.1.refs_0_, f32[34,88,256]{2,1,0:T(8,128)} %pad_maximum_fusion.refs_1_, f32[33,64,128]{2,1,0:T(8,128)} %refs_2_.2), custom_call_target="tpu_custom_call" | custom-call | tf_op jit(solution)/shard_map/pallas_call | solution.py:106
  (80 shorter events, 21.3 us)
Async XLA Ops:
  3.8 50.6 %collective-permute-start = (f32[42,10,128]{2,1,0:T(8,128)}, f32[42,10,128]{2,1,0:T(8,128)S(1)}, u32[]{:S(2)}, u32[]{:S(2)}) collective-permute-start(f32[42,10,128]{2,1,0:T(8,128)} %get-tuple-element.6), channel_id=1, source_target_pairs={{0,192},{4,196},{8,200},{12,204},{16,208},{20,212},{24,216},{28,22... | collective-permute-start | bytes 645128 | tf_op jit(solution)/shard_map/ppermute | solution.py:41
  4.5 49.9 %collective-permute-start.1 = (f32[42,10,128]{2,1,0:T(8,128)}, f32[42,10,128]{2,1,0:T(8,128)S(1)}, u32[]{:S(2)}, u32[]{:S(2)}) collective-permute-start(f32[42,10,128]{2,1,0:T(8,128)} %get-tuple-element.7), channel_id=1, source_target_pairs={{0,64},{4,68},{8,72},{12,76},{16,80},{20,84},{24,88},{28,92},{32,9... | collective-permute-start | bytes 645128 | tf_op jit(solution)/shard_map/ppermute | solution.py:41
  8.3 15.9 %collective-permute-start.3 = (f32[42,10,10]{2,1,0:T(8,128)}, f32[42,10,10]{2,1,0:T(8,128)}, u32[]{:S(2)}, u32[]{:S(2)}) collective-permute-start(f32[42,10,10]{2,1,0:T(8,128)} %get-tuple-element.10), channel_id=1, source_target_pairs={{4,192},{8,196},{12,200},{16,204},{20,208},{24,212},{28,216},{32,2... | collective-permute-start | bytes 50408 | tf_op jit(solution)/shard_map/ppermute | solution.py:41
  10.7 9.0 %copy-start.15 = (s32[2048]{0:T(1024)S(1)}, s32[2048]{0:T(1024)}, u32[]{:S(2)}) copy-start(s32[2048]{0:T(1024)} %param.14) | copy-start | bytes 24580
  11.9 20.0 %collective-permute-start.5 = (f32[42,64,10]{1,0,2:T(8,128)}, f32[42,64,10]{1,0,2:T(8,128)S(1)}, u32[]{:S(2)}, u32[]{:S(2)}) collective-permute-start(f32[42,64,10]{1,0,2:T(8,128)} %copy.29), channel_id=1, source_target_pairs={{0,4},{4,8},{8,12},{12,16},{16,20},{20,24},{24,28},{28,32},{32,36}... | collective-permute-start | bytes 322568 | tf_op jit(solution)/shard_map/ppermute | solution.py:41
  17.8 18.3 %collective-permute-start.2 = (f32[42,64,10]{1,0,2:T(8,128)S(1)}, f32[42,64,10]{1,0,2:T(8,128)S(1)}, u32[]{:S(2)}, u32[]{:S(2)}) collective-permute-start(f32[42,64,10]{1,0,2:T(8,128)S(1)} %copy.27), channel_id=1, source_target_pairs={{4,0},{8,4},{12,8},{16,12},{20,16},{24,20},{28,24},{32,28},{36,32}... | collective-permute-start | bytes 322568 | tf_op jit(solution)/shard_map/ppermute | solution.py:41
  24.2 25.1 %collective-permute-start.6 = (f32[42,10,10]{2,1,0:T(8,128)}, f32[42,10,10]{2,1,0:T(8,128)}, u32[]{:S(2)}, u32[]{:S(2)}) collective-permute-start(f32[42,10,10]{2,1,0:T(8,128)} %get-tuple-element.11), channel_id=1, source_target_pairs={{0,196},{4,200},{8,204},{12,208},{16,212},{20,216},{24,220},{28,22... | collective-permute-start | bytes 50408 | tf_op jit(solution)/shard_map/ppermute | solution.py:41
  31.9 10.1 %copy-start.12 = (f32[42,64,10]{1,0,2:T(8,128)}, f32[42,64,10]{1,0,2:T(8,128)S(1)}, u32[]{:S(2)}) copy-start(f32[42,64,10]{1,0,2:T(8,128)S(1)} %collective-permute-done.5) | copy-start | bytes 322564
  31.9 19.2 %collective-permute-start.4 = (f32[42,10,10]{2,1,0:T(8,128)}, f32[42,10,10]{2,1,0:T(8,128)}, u32[]{:S(2)}, u32[]{:S(2)}) collective-permute-start(f32[42,10,10]{2,1,0:T(8,128)} %get-tuple-element.12), channel_id=1, source_target_pairs={{4,64},{8,68},{12,72},{16,76},{20,80},{24,84},{28,88},{32,92},{36,... | collective-permute-start | bytes 50408 | tf_op jit(solution)/shard_map/ppermute | solution.py:41
  36.1 6.0 %copy-start.13 = (f32[42,64,10]{1,0,2:T(8,128)}, f32[42,64,10]{1,0,2:T(8,128)S(1)}, u32[]{:S(2)}) copy-start(f32[42,64,10]{1,0,2:T(8,128)S(1)} %collective-permute-done.2) | copy-start | bytes 322564
  36.1 18.3 %collective-permute-start.7 = (f32[42,10,10]{2,1,0:T(8,128)}, f32[42,10,10]{2,1,0:T(8,128)}, u32[]{:S(2)}, u32[]{:S(2)}) collective-permute-start(f32[42,10,10]{2,1,0:T(8,128)} %get-tuple-element.13), channel_id=1, source_target_pairs={{0,68},{4,72},{8,76},{12,80},{16,84},{20,88},{24,92},{28,96},{32,1... | collective-permute-start | bytes 50408 | tf_op jit(solution)/shard_map/ppermute | solution.py:41
  42.1 12.3 %copy-start.8 = (f32[88,256]{1,0:T(8,128)}, f32[88,256]{1,0:T(8,128)S(1)}, u32[]{:S(2)}) copy-start(f32[88,256]{1,0:T(8,128)S(1)} %pad.25.clone) | copy-start | bytes 270340
  42.1 12.3 %copy-start.2 = (f32[33,64,128]{2,1,0:T(8,128)S(1)}, f32[33,64,128]{2,1,0:T(8,128)}, u32[]{:S(2)}) copy-start(f32[33,64,128]{2,1,0:T(8,128)} %refs_2_.2) | copy-start | bytes 3244036
  42.1 12.3 %copy-start.7 = (f32[4,64,128]{2,1,0:T(8,128)S(1)}, f32[4,64,128]{2,1,0:T(8,128)}, u32[]{:S(2)}) copy-start(f32[4,64,128]{2,1,0:T(8,128)} %refs_2_.3) | copy-start | bytes 393220
  42.1 12.3 %copy-start.9 = (f32[4,64,128]{2,1,0:T(8,128)S(1)}, f32[4,64,128]{2,1,0:T(8,128)}, u32[]{:S(2)}) copy-start(f32[4,64,128]{2,1,0:T(8,128)} %param.12) | copy-start | bytes 393220
  66.8 55.0 %copy-start.3 = (bf16[4,33,64,128]{3,2,1,0:T(8,128)(2,1)S(1)}, bf16[4,33,64,128]{3,2,1,0:T(8,128)(2,1)}, u32[]{:S(2)}) copy-start(bf16[4,33,64,128]{3,2,1,0:T(8,128)(2,1)} %param.10) | copy-start | bytes 6488068
  66.8 55.0 %copy-start.10 = (f32[4,64,128]{2,1,0:T(8,128)S(1)}, f32[4,64,128]{2,1,0:T(8,128)}, u32[]{:S(2)}) copy-start(f32[4,64,128]{2,1,0:T(8,128)} %shard_map.105) | copy-start | bytes 393220
  135.2 19.9 %copy-start.16 = (f32[2048]{0:T(1024)S(1)}, f32[2048]{0:T(1024)}, u32[]{:S(2)}) copy-start(f32[2048]{0:T(1024)} %param.17) | copy-start | bytes 24580
  135.2 19.9 %copy-start.17 = (f32[2048]{0:T(1024)S(1)}, f32[2048]{0:T(1024)}, u32[]{:S(2)}) copy-start(f32[2048]{0:T(1024)} %param.16) | copy-start | bytes 24580
  135.3 31.5 %copy-start.4 = (bf16[4,33,64,128]{3,2,1,0:T(8,128)(2,1)S(1)}, bf16[4,33,64,128]{3,2,1,0:T(8,128)(2,1)}, u32[]{:S(2)}) copy-start(bf16[4,33,64,128]{3,2,1,0:T(8,128)(2,1)} %param.10) | copy-start | bytes 6488068
  167.2 6.0 %copy-start.5 = (f32[4,64,128]{2,1,0:T(8,128)}, f32[4,64,128]{2,1,0:T(8,128)S(1)}, u32[]{:S(2)}) copy-start(f32[4,64,128]{2,1,0:T(8,128)S(1)} %broadcast_multiply_fusion.1) | copy-start | bytes 393220
  168.1 52.5 %collective-permute-start.8 = (f32[37,10,128]{2,1,0:T(8,128)}, f32[37,10,128]{2,1,0:T(8,128)}, u32[]{:S(2)}, u32[]{:S(2)}) collective-permute-start(f32[37,10,128]{2,1,0:T(8,128)} %get-tuple-element.14), channel_id=1, source_target_pairs={{0,192},{4,196},{8,200},{12,204},{16,208},{20,212},{24,216},{28,22... | collective-permute-start | bytes 568328 | tf_op jit(solution)/shard_map/ppermute | solution.py:41
  168.6 52.0 %collective-permute-start.9 = (f32[37,10,128]{2,1,0:T(8,128)}, f32[37,10,128]{2,1,0:T(8,128)}, u32[]{:S(2)}, u32[]{:S(2)}) collective-permute-start(f32[37,10,128]{2,1,0:T(8,128)} %get-tuple-element.15), channel_id=1, source_target_pairs={{0,64},{4,68},{8,72},{12,76},{16,80},{20,84},{24,88},{28,92},{32,9... | collective-permute-start | bytes 568328 | tf_op jit(solution)/shard_map/ppermute | solution.py:41
  174.3 6.3 %copy-start.6 = (f32[4,64,128]{2,1,0:T(8,128)S(1)}, f32[4,64,128]{2,1,0:T(8,128)}, u32[]{:S(2)}) copy-start(f32[4,64,128]{2,1,0:T(8,128)} %copy-done.5) | copy-start | bytes 393220
  174.7 22.0 %collective-permute-start.13 = (f32[37,64,10]{1,0,2:T(8,128)S(1)}, f32[37,64,10]{1,0,2:T(8,128)S(1)}, u32[]{:S(2)}, u32[]{:S(2)}) collective-permute-start(f32[37,64,10]{1,0,2:T(8,128)S(1)} %copy.33), channel_id=1, source_target_pairs={{0,4},{4,8},{8,12},{12,16},{16,20},{20,24},{24,28},{28,32},{32,36}... | collective-permute-start | bytes 284168 | tf_op jit(solution)/shard_map/ppermute | solution.py:41
  176.7 26.8 %collective-permute-start.10 = (f32[37,64,10]{1,0,2:T(8,128)}, f32[37,64,10]{1,0,2:T(8,128)S(1)}, u32[]{:S(2)}, u32[]{:S(2)}) collective-permute-start(f32[37,64,10]{1,0,2:T(8,128)} %copy.31), channel_id=1, source_target_pairs={{4,0},{8,4},{12,8},{16,12},{20,16},{24,20},{28,24},{32,28},{36,32}... | collective-permute-start | bytes 284168 | tf_op jit(solution)/shard_map/ppermute | solution.py:41
  181.7 13.1 %collective-permute-start.11 = (f32[37,10,10]{2,1,0:T(8,128)S(1)}, f32[37,10,10]{2,1,0:T(8,128)S(1)}, u32[]{:S(2)}, u32[]{:S(2)}) collective-permute-start(f32[37,10,10]{2,1,0:T(8,128)S(1)} %get-tuple-element.18), channel_id=1, source_target_pairs={{4,192},{8,196},{12,200},{16,204},{20,208},{24,212},{28,216},{32,2... | collective-permute-start | bytes 44408 | tf_op jit(solution)/shard_map/ppermute | solution.py:41
  194.8 8.6 %copy-start.11 = (f32[37,10,10]{2,1,0:T(8,128)}, f32[37,10,10]{2,1,0:T(8,128)S(1)}, u32[]{:S(2)}) copy-start(f32[37,10,10]{2,1,0:T(8,128)S(1)} %collective-permute-done.11) | copy-start | bytes 44404
  194.8 20.2 %collective-permute-start.12 = (f32[37,10,10]{2,1,0:T(8,128)}, f32[37,10,10]{2,1,0:T(8,128)}, u32[]{:S(2)}, u32[]{:S(2)}) collective-permute-start(f32[37,10,10]{2,1,0:T(8,128)} %get-tuple-element.19), channel_id=1, source_target_pairs={{4,64},{8,68},{12,72},{16,76},{20,80},{24,84},{28,88},{32,92},{36,... | collective-permute-start | bytes 44408 | tf_op jit(solution)/shard_map/ppermute | solution.py:41
  196.8 6.7 %copy-start.14 = (f32[37,64,10]{1,0,2:T(8,128)}, f32[37,64,10]{1,0,2:T(8,128)S(1)}, u32[]{:S(2)}) copy-start(f32[37,64,10]{1,0,2:T(8,128)S(1)} %collective-permute-done.13) | copy-start | bytes 284164
  196.8 18.3 %collective-permute-start.15 = (f32[37,10,10]{2,1,0:T(8,128)}, f32[37,10,10]{2,1,0:T(8,128)}, u32[]{:S(2)}, u32[]{:S(2)}) collective-permute-start(f32[37,10,10]{2,1,0:T(8,128)} %get-tuple-element.20), channel_id=1, source_target_pairs={{0,68},{4,72},{8,76},{12,80},{16,84},{20,88},{24,92},{28,96},{32,1... | collective-permute-start | bytes 44408 | tf_op jit(solution)/shard_map/ppermute | solution.py:41
  203.5 17.1 %collective-permute-start.14 = (f32[37,10,10]{2,1,0:T(8,128)}, f32[37,10,10]{2,1,0:T(8,128)}, u32[]{:S(2)}, u32[]{:S(2)}) collective-permute-start(f32[37,10,10]{2,1,0:T(8,128)} %get-tuple-element.21), channel_id=1, source_target_pairs={{0,196},{4,200},{8,204},{12,208},{16,212},{20,216},{24,220},{28,22... | collective-permute-start | bytes 44408 | tf_op jit(solution)/shard_map/ppermute | solution.py:41
  (2 other events, 3.1 us)
